TPU v7x, 128 devices: a whole 4x4x4 slice. The times are simulated.
128 devices in a mesh: head: 8 (over z_hi, x), frame: 16 (over z_lo, y, core).
Axes of the slice: x: 4, y: 4, z: 4 (z_hi: 2, z_lo: 2; z = z_hi * 2 + z_lo), core: 2. Of those that a mesh axis runs over, the one named last changes fastest.
Arguments:
- query_tok: bfloat16 [12288, 3072], P('frame', 'head'), may hold values from -200 to 200
- key_tok: bfloat16 [12288, 3072], P('frame', 'head'), may hold values from -8 to 8
- value_tok: bfloat16 [12288, 3072], P('frame', 'head'), may hold values from -6 to 6
- head_span: int32 [24], P('head'), may hold values from 0 to 3
- out_weight: bfloat16 [3072, 3072], P('head'), may hold values from -0.109375 to 0.109375
Outputs:
- projected: bfloat16 [12288, 3072], P('frame', 'head')
All inputs are finite; a program needn't handle non-finite values.
Results may differ from a plain program's by a relative error of at most 0.012.
Values may be sent and summed in bfloat16 or wider, within the bound.
A program may use at most 64 MiB of HBM per device.

v0:
```python
import jax
import jax.numpy as jnp
from jax import lax
from jax.sharding import PartitionSpec as P

HD = 128
FRAME_TOK = 384


def from_behind(value, axis, steps):
    count = lax.axis_size(axis)
    leading, last = (max(0, -steps), min(count, count - steps))
    return lax.ppermute(value, axis, [(source, source + steps) for source in range(leading, last)])


def attend_frame(query_frame, key_rows, value_rows, frame_pos, head_span, frame_count):
    scale = 1.0 / HD**0.5
    scores = (
        jnp.einsum("qhd,khd->hqk", query_frame, key_rows, preferred_element_type=jnp.float32)
        * scale
    )
    offsets = jnp.arange(7, dtype=jnp.int32) - 3
    allowed = (
        (jnp.abs(offsets)[None, :] <= head_span[:, None])
        & (frame_pos + offsets >= 0)[None, :]
        & (frame_pos + offsets < frame_count)[None, :]
    )
    visible = jnp.repeat(allowed, FRAME_TOK, axis=1)[:, None, :]
    scores = jnp.where(visible, scores, -1e30)
    rowmax = jnp.max(scores, axis=2, keepdims=True)
    weights = jnp.where(visible, jnp.exp(scores - rowmax), 0.0)
    total = jnp.sum(weights, axis=2)
    probs = weights.astype(jnp.bfloat16)
    mixed = jnp.einsum("hqk,khd->qhd", probs, value_rows, preferred_element_type=jnp.float32)
    return (mixed / jnp.transpose(total)[:, :, None]).astype(jnp.bfloat16)


def body(query_tok, key_tok, value_tok, head_span, out_weight):
    local_frames = key_tok.shape[0] // FRAME_TOK
    heads_here = head_span.shape[0]
    width = key_tok.shape[1]
    key_local = key_tok.reshape(local_frames, FRAME_TOK, width)
    value_local = value_tok.reshape(local_frames, FRAME_TOK, width)
    received = {}
    for offset in (1, -1):
        received[offset] = from_behind((key_local, value_local), "frame", offset)
    for offset in (2, -2):
        received[offset] = from_behind((key_local, value_local), "frame", offset)
    lower = (received[2][0][1:2], received[2][1][1:2])
    upper = (received[-2][0][0:1], received[-2][1][0:1])
    key_window = jnp.concatenate(
        [lower[0], received[1][0], key_local, received[-1][0], upper[0]], axis=0
    )
    value_window = jnp.concatenate(
        [lower[1], received[1][1], value_local, received[-1][1], upper[1]], axis=0
    )
    frame_count = lax.axis_size("frame") * local_frames
    first_frame = lax.axis_index("frame") * local_frames
    query_all = query_tok.reshape(local_frames, FRAME_TOK, heads_here, HD)
    outputs = []
    for local in range(local_frames):
        key_rows = key_window[local : local + 7].reshape(7 * FRAME_TOK, heads_here, HD)
        value_rows = value_window[local : local + 7].reshape(7 * FRAME_TOK, heads_here, HD)
        outputs.append(
            attend_frame(
                query_all[local], key_rows, value_rows, first_frame + local, head_span, frame_count
            )
        )
    attended = jnp.concatenate(outputs, axis=0).reshape(local_frames * FRAME_TOK, width)
    terms = jnp.dot(attended, out_weight, preferred_element_type=jnp.float32)
    return lax.psum_scatter(terms.astype(jnp.bfloat16), "head", scatter_dimension=1, tiled=True)


def solution(mesh):
    return jax.shard_map(
        body,
        mesh=mesh,
        in_specs=(
            P("frame", "head"),
            P("frame", "head"),
            P("frame", "head"),
            P("head"),
            P("head", None),
        ),
        out_specs=P("frame", "head"),
        check_vma=False,
    )
```

profile of v0, /device:TPU:24, one launch (start us, length us, event | category | flops | bytes accessed | tf_op | source)
XLA Modules:
  0.0 227.2 jit_solution(2747761536581647858)
XLA Ops:
  6.5 2.4 %copy.38 = bf16[2,384,384]{1,0,2:T(2,128)(2,1)S(1)} copy(bf16[2,384,384]{2,1,0:T(8,128)(2,1)} %bitcast.78) | data formatting | bytes 1179648 | tf_op jit(solution)/shard_map/reshape | solution.py:42
  8.9 2.7 %collective-permute-start.7 = (bf16[2,384,384]{1,0,2:T(2,128)(2,1)S(1)}, bf16[2,384,384]{1,0,2:T(2,128)(2,1)}, u32[]{:S(2)}, u32[]{:S(2)}) collective-permute-start(bf16[2,384,384]{1,0,2:T(2,128)(2,1)S(1)} %copy.38), channel_id=1, source_target_pairs={{2,0},{3,1},{4,2},{5,3},{6,4},{7,5},{8,6},{9,7},{10,8},{11,9},{12,... | collective-permute-start | bytes 1769480 | tf_op jit(solution)/shard_map/ppermute | solution.py:13
  11.6 1.9 collective-permute-start.5
  13.5 2.4 %collective-permute-start.4 = (bf16[2,384,384]{1,0,2:T(2,128)(2,1)S(1)}, bf16[2,384,384]{1,0,2:T(2,128)(2,1)}, u32[]{:S(2)}, u32[]{:S(2)}) collective-permute-start(bf16[2,384,384]{1,0,2:T(2,128)(2,1)S(1)} %copy.38), channel_id=1, source_target_pairs={{0,1},{1,2},{2,3},{3,4},{4,5},{5,6},{6,7},{7,8},{8,9},{9,10},{10,1... | collective-permute-start | bytes 1769480 | tf_op jit(solution)/shard_map/ppermute | solution.py:13
  15.9 5.3 %collective-permute-start.3 = (bf16[2,384,384]{1,0,2:T(2,128)(2,1)S(1)}, bf16[2,384,384]{1,0,2:T(2,128)(2,1)}, u32[]{:S(2)}, u32[]{:S(2)}) collective-permute-start(bf16[2,384,384]{1,0,2:T(2,128)(2,1)S(1)} %copy.38), channel_id=1, source_target_pairs={{0,2},{1,3},{2,4},{3,5},{4,6},{5,7},{6,8},{7,9},{8,10},{9,11},{10,... | collective-permute-start | bytes 1769480 | tf_op jit(solution)/shard_map/ppermute | solution.py:13
  21.3 2.3 copy.34
  30.0 4.0 %collective-permute-done.5 = bf16[2,384,384]{1,0,2:T(2,128)(2,1)} collective-permute-done((bf16[2,384,384]{1,0,2:T(2,128)(2,1)S(1)}, bf16[2,384,384]{1,0,2:T(2,128)(2,1)}, u32[]{:S(2)}, u32[]{:S(2)}) %collective-permute-start.5) | collective-permute-done | bytes 589856 | tf_op jit(solution)/shard_map/ppermute | solution.py:13
  34.0 5.8 %collective-permute-start.1 = (bf16[2,384,384]{1,0,2:T(2,128)(2,1)S(1)}, bf16[2,384,384]{1,0,2:T(2,128)(2,1)}, u32[]{:S(2)}, u32[]{:S(2)}) collective-permute-start(bf16[2,384,384]{1,0,2:T(2,128)(2,1)S(1)} %copy.34), channel_id=1, source_target_pairs={{0,1},{1,2},{2,3},{3,4},{4,5},{5,6},{6,7},{7,8},{8,9},{9,10},{10,1... | collective-permute-start | bytes 1769480 | tf_op jit(solution)/shard_map/ppermute | solution.py:13
  39.8 2.7 %collective-permute-start = (bf16[2,384,384]{1,0,2:T(2,128)(2,1)S(1)}, bf16[2,384,384]{1,0,2:T(2,128)(2,1)}, u32[]{:S(2)}, u32[]{:S(2)}) collective-permute-start(bf16[2,384,384]{1,0,2:T(2,128)(2,1)S(1)} %copy.34), channel_id=1, source_target_pairs={{0,2},{1,3},{2,4},{3,5},{4,6},{5,7},{6,8},{7,9},{8,10},{9,11},{10,... | collective-permute-start | bytes 1769480 | tf_op jit(solution)/shard_map/ppermute | solution.py:13
  42.6 1.9 fusion.57
  49.9 8.4 %pad_maximum_fusion.1 = (bf16[7,384,384]{1,0,2:T(8,128)(2,1)}, bf16[7,384,384]{1,0,2:T(8,128)(2,1)}) fusion(bf16[2,384,384]{1,0,2:T(2,128)(2,1)} %collective-permute-done.5, bf16[2,384,384]{1,0,2:T(2,128)(2,1)S(1)} %copy.38, bf16[2,384,384]{1,0,2:T(2,128)(2,1)} %collective-permute-done.4, bf16[1,384,384]{1,0,2:T(2,128)(2,1)S(1)} %slice.35, ...), kind=kLoop, calls=%fused_computation.26 | loop fusion | flops 16515072 | bytes 6488064 | tf_op jit(solution)/shard_map/concatenate | solution.py:51
  58.3 5.0 %reshape.55 = bf16[2688,3,128]{0,2,1:T(8,128)(2,1)} reshape(bf16[7,384,384]{1,0,2:T(8,128)(2,1)} %get-tuple-element.5) | data formatting | bytes 4128768 | tf_op jit(solution)/shard_map/reshape | solution.py:62
  65.1 8.1 %pad_maximum_fusion = (bf16[7,384,384]{1,0,2:T(8,128)(2,1)}, bf16[7,384,384]{1,0,2:T(8,128)(2,1)}) fusion(bf16[2,384,384]{1,0,2:T(2,128)(2,1)} %collective-permute-done.2, bf16[2,384,384]{1,0,2:T(2,128)(2,1)S(1)} %copy.34, bf16[2,384,384]{1,0,2:T(2,128)(2,1)} %collective-permute-done.1, bf16[1,384,384]{1,0,2:T(2,128)(2,1)S(1)} %slice.34, ...), kind=kLoop, calls=%fused_computation.25 | loop fusion | flops 16515072 | bytes 6488064 | tf_op jit(solution)/shard_map/concatenate | solution.py:54
  73.2 5.0 %reshape.53 = bf16[2688,3,128]{0,2,1:T(8,128)(2,1)} reshape(bf16[7,384,384]{1,0,2:T(8,128)(2,1)} %get-tuple-element.7) | data formatting | bytes 4128768 | tf_op jit(solution)/shard_map/reshape | solution.py:63
  78.2 5.1 %reshape.56 = bf16[2688,3,128]{0,2,1:T(8,128)(2,1)} reshape(bf16[7,384,384]{1,0,2:T(8,128)(2,1)} %get-tuple-element.8) | data formatting | bytes 4128768 | tf_op jit(solution)/shard_map/reshape | solution.py:63
  83.3 5.0 %reshape.57 = bf16[2688,3,128]{0,2,1:T(8,128)(2,1)} reshape(bf16[7,384,384]{1,0,2:T(8,128)(2,1)} %get-tuple-element.6) | data formatting | bytes 4128768 | tf_op jit(solution)/shard_map/reshape | solution.py:62
  88.3 8.7 %fusion.58 = (f32[3,384]{1,0:T(4,128)S(1)}, bf16[3,384,2688]{1,2,0:T(8,128)(2,1)}) fusion(pred[3,2688]{1,0:T(4,128)(4,1)S(1)} %bitcast.85, bf16[2688,3,128]{0,2,1:T(8,128)(2,1)} %reshape.57, bf16[384,3,128]{0,2,1:T(8,128)(2,1)S(1)} %bitcast.83), kind=kOutput, calls=%fused_computation.57 | convolution fusion | flops 811305600 | bytes 8565120 | tf_op jit(solution)/shard_map/sub | solution.py:31
  97.0 4.7 %fusion.41 = bf16[384,3,128]{0,2,1:T(8,128)(2,1)S(1)} fusion(bf16[2688,3,128]{0,2,1:T(8,128)(2,1)} %reshape.56, bf16[3,384,2688]{1,2,0:T(8,128)(2,1)} %get-tuple-element.14, f32[384,3]{0,1:T(4,128)S(1)} %bitcast.86), kind=kOutput, calls=%fused_computation.36 | convolution fusion | flops 793018368 | bytes 8557056 | tf_op jit(solution)/shard_map/hqk,khd->qhd/dot_general | solution.py:34
  101.8 8.7 %fusion.59 = (f32[3,384]{1,0:T(4,128)S(1)}, bf16[3,384,2688]{1,2,0:T(8,128)(2,1)}) fusion(pred[3,2688]{1,0:T(4,128)(4,1)S(1)} %bitcast.84, bf16[2688,3,128]{0,2,1:T(8,128)(2,1)} %reshape.55, bf16[384,3,128]{0,2,1:T(8,128)(2,1)S(1)} %bitcast.82), kind=kOutput, calls=%fused_computation.58 | convolution fusion | flops 811305600 | bytes 8565120 | tf_op jit(solution)/shard_map/sub | solution.py:31
  110.5 4.7 %fusion.38 = bf16[384,3,128]{0,2,1:T(8,128)(2,1)S(1)} fusion(bf16[2688,3,128]{0,2,1:T(8,128)(2,1)} %reshape.53, bf16[3,384,2688]{1,2,0:T(8,128)(2,1)} %get-tuple-element.16, f32[384,3]{0,1:T(4,128)S(1)} %bitcast.87), kind=kOutput, calls=%fused_computation.35 | convolution fusion | flops 793018368 | bytes 8557056 | tf_op jit(solution)/shard_map/hqk,khd->qhd/dot_general | solution.py:34
  115.3 4.4 %convolution_convert_fusion = bf16[768,3072]{1,0:T(8,128)(2,1)} fusion(bf16[768,384]{0,1:T(8,128)(2,1)S(1)} %bitcast.81, bf16[384,3072]{1,0:T(8,128)(2,1)S(1)} %copy-done), kind=kOutput, calls=%fused_computation.24 | convolution fusion | flops 1814298624 | bytes 7667712 | tf_op jit(solution)/shard_map/dot_general | solution.py:70
  119.7 6.6 %copy.60 = bf16[768,3072]{0,1:T(8,128)(2,1)} copy(bf16[768,3072]{1,0:T(8,128)(2,1)} %convolution_convert_fusion) | data formatting | bytes 9437184
  126.3 91.9 %reduce-scatter.4.cloned.1.call-done = bf16[384,768]{1,0:T(8,128)(2,1)} async-done(((bf16[3072,768]{1,0:T(8,128)(2,1)}), bf16[384,768]{1,0:T(8,128)(2,1)}) %reduce-scatter.4.cloned.1.call-update) | async-done | bytes 589840
  218.2 2.1 copy.61
  (32 shorter events, 13.7 us)
Async XLA Ops:
  6.5 108.7 %copy-start = (bf16[384,3072]{1,0:T(8,128)(2,1)S(1)}, bf16[384,3072]{1,0:T(8,128)(2,1)}, u32[]{:S(2)}) copy-start(bf16[384,3072]{1,0:T(8,128)(2,1)} %param.9) | copy-start | bytes 7077892
  6.5 211.7 %reduce-scatter.4.cloned.1.call-start = ((), (), s32[]{:S(2)}) async-start(), calls=%async_computation.1 | async-start | bytes 5308416
  8.9 19.2 %collective-permute-start.7 = (bf16[2,384,384]{1,0,2:T(2,128)(2,1)S(1)}, bf16[2,384,384]{1,0,2:T(2,128)(2,1)}, u32[]{:S(2)}, u32[]{:S(2)}) collective-permute-start(bf16[2,384,384]{1,0,2:T(2,128)(2,1)S(1)} %copy.38), channel_id=1, source_target_pairs={{2,0},{3,1},{4,2},{5,3},{6,4},{7,5},{8,6},{9,7},{10,8},{11,9},{12,... | collective-permute-start | bytes 1769480 | tf_op jit(solution)/shard_map/ppermute | solution.py:13
  11.6 22.4 %collective-permute-start.5 = (bf16[2,384,384]{1,0,2:T(2,128)(2,1)S(1)}, bf16[2,384,384]{1,0,2:T(2,128)(2,1)}, u32[]{:S(2)}, u32[]{:S(2)}) collective-permute-start(bf16[2,384,384]{1,0,2:T(2,128)(2,1)S(1)} %copy.38), channel_id=1, source_target_pairs={{1,0},{2,1},{3,2},{4,3},{5,4},{6,5},{7,6},{8,7},{9,8},{10,9},{11,1... | collective-permute-start | bytes 1769480 | tf_op jit(solution)/shard_map/ppermute | solution.py:13
  13.5 36.4 %collective-permute-start.4 = (bf16[2,384,384]{1,0,2:T(2,128)(2,1)S(1)}, bf16[2,384,384]{1,0,2:T(2,128)(2,1)}, u32[]{:S(2)}, u32[]{:S(2)}) collective-permute-start(bf16[2,384,384]{1,0,2:T(2,128)(2,1)S(1)} %copy.38), channel_id=1, source_target_pairs={{0,1},{1,2},{2,3},{3,4},{4,5},{5,6},{6,7},{7,8},{8,9},{9,10},{10,1... | collective-permute-start | bytes 1769480 | tf_op jit(solution)/shard_map/ppermute | solution.py:13
  15.9 23.9 %collective-permute-start.3 = (bf16[2,384,384]{1,0,2:T(2,128)(2,1)S(1)}, bf16[2,384,384]{1,0,2:T(2,128)(2,1)}, u32[]{:S(2)}, u32[]{:S(2)}) collective-permute-start(bf16[2,384,384]{1,0,2:T(2,128)(2,1)S(1)} %copy.38), channel_id=1, source_target_pairs={{0,2},{1,3},{2,4},{3,5},{4,6},{5,7},{6,8},{7,9},{8,10},{9,11},{10,... | collective-permute-start | bytes 1769480 | tf_op jit(solution)/shard_map/ppermute | solution.py:13
  23.5 41.6 %collective-permute-start.6 = (bf16[2,384,384]{1,0,2:T(2,128)(2,1)S(1)}, bf16[2,384,384]{1,0,2:T(2,128)(2,1)}, u32[]{:S(2)}, u32[]{:S(2)}) collective-permute-start(bf16[2,384,384]{1,0,2:T(2,128)(2,1)S(1)} %copy.34), channel_id=1, source_target_pairs={{2,0},{3,1},{4,2},{5,3},{6,4},{7,5},{8,6},{9,7},{10,8},{11,9},{12,... | collective-permute-start | bytes 1769480 | tf_op jit(solution)/shard_map/ppermute | solution.py:13
  28.1 37.0 %collective-permute-start.2 = (bf16[2,384,384]{1,0,2:T(2,128)(2,1)S(1)}, bf16[2,384,384]{1,0,2:T(2,128)(2,1)}, u32[]{:S(2)}, u32[]{:S(2)}) collective-permute-start(bf16[2,384,384]{1,0,2:T(2,128)(2,1)S(1)} %copy.34), channel_id=1, source_target_pairs={{1,0},{2,1},{3,2},{4,3},{5,4},{6,5},{7,6},{8,7},{9,8},{10,9},{11,1... | collective-permute-start | bytes 1769480 | tf_op jit(solution)/shard_map/ppermute | solution.py:13
  34.0 31.1 %collective-permute-start.1 = (bf16[2,384,384]{1,0,2:T(2,128)(2,1)S(1)}, bf16[2,384,384]{1,0,2:T(2,128)(2,1)}, u32[]{:S(2)}, u32[]{:S(2)}) collective-permute-start(bf16[2,384,384]{1,0,2:T(2,128)(2,1)S(1)} %copy.34), channel_id=1, source_target_pairs={{0,1},{1,2},{2,3},{3,4},{4,5},{5,6},{6,7},{7,8},{8,9},{9,10},{10,1... | collective-permute-start | bytes 1769480 | tf_op jit(solution)/shard_map/ppermute | solution.py:13
  39.8 23.6 %collective-permute-start = (bf16[2,384,384]{1,0,2:T(2,128)(2,1)S(1)}, bf16[2,384,384]{1,0,2:T(2,128)(2,1)}, u32[]{:S(2)}, u32[]{:S(2)}) collective-permute-start(bf16[2,384,384]{1,0,2:T(2,128)(2,1)S(1)} %copy.34), channel_id=1, source_target_pairs={{0,2},{1,3},{2,4},{3,5},{4,6},{5,7},{6,8},{7,9},{8,10},{9,11},{10,... | collective-permute-start | bytes 1769480 | tf_op jit(solution)/shard_map/ppermute | solution.py:13
  78.2 10.1 %copy-start.2 = (bf16[384,384]{0,1:T(8,128)(2,1)S(1)}, bf16[384,384]{0,1:T(8,128)(2,1)}, u32[]{:S(2)}) copy-start(bf16[384,384]{0,1:T(8,128)(2,1)} %copy.63) | copy-start | bytes 884740
  78.2 10.1 %copy-start.3 = (pred[1,3,7,384]{3,1,2,0:T(4,128)(4,1)S(1)}, pred[1,3,7,384]{3,1,2,0:T(4,128)(4,1)}, u32[]{:S(2)}) copy-start(pred[1,3,7,384]{3,1,2,0:T(4,128)(4,1)} %copy.65) | copy-start | bytes 24196
  97.0 4.7 %copy-start.1 = (bf16[384,384]{0,1:T(8,128)(2,1)S(1)}, bf16[384,384]{0,1:T(8,128)(2,1)}, u32[]{:S(2)}) copy-start(bf16[384,384]{0,1:T(8,128)(2,1)} %copy.62) | copy-start | bytes 884740
Sparse Core Ops, SparseCore 0:
  126.5 91.7 reduce-scatter.3
where the time goes:
time: 229 us; the launch traced here: 227 us
  waiting for transfers between devices  97 us (42%)
  local copies, waits for them, and re-layouts  43.4 us (19%)
  matrix products  31.3 us (14%)
  starting transfers between devices  24.6 us (11%)
  other arithmetic  17.3 us (8%)
  between operations  13.6 us (6%)
    unnamed x2, waiting for transfers between devices  91.9 us
    ppermute x8, starting transfers between devices, from_behind(): lax.ppermute(value, axis, [(source, source + steps) for source in range(l...  24.6 us
    sub x2, matrix products, attend_frame(): weights = jnp.where(visible, jnp.exp(scores - rowmax), 0.0)  17.5 us
    unnamed x16, local copies, waits for them, and re-layouts  13.3 us
    reshape x2, local copies, waits for them, and re-layouts, body(): value_window[local:local + 7].reshape(7 * FRAME_TOK, heads_here, HD)  10.1 us
    reshape x2, local copies, waits for them, and re-layouts, body(): key_window[local:local + 7].reshape(7 * FRAME_TOK, heads_here, HD)  10 us
    dot_general x2, matrix products, attend_frame(): jnp.einsum('hqk,khd->qhd', probs, value_rows, preferred_element_type=jnp....  9.4 us
    concatenate x1, other arithmetic, body(): jnp.concatenate([lower[0], received[1][0], key_local, received[-1][0], up...  8.41 us
  transfers between devices with their start and end apart: 9, of which 3 were waited for; matrix products, arithmetic and copies ran while one was open for 12% of the time, Pallas kernels for 0%

commit v1 on v0

v1 whole, which is shorter than its diff:
```python
import functools
import math

import jax
import jax.numpy as jnp
from jax import lax
from jax.experimental import pallas as pl
from jax.experimental.pallas import tpu as pltpu
from jax.sharding import PartitionSpec as P

MESH = pl.DeviceIdType.MESH
HD = 128
T = 384
HALF = T // 2
G = 384
NH = 3
NX = 4
F32 = jnp.float32
BF16 = jnp.bfloat16
SCALE = math.log2(math.e) / math.sqrt(HD)
HIDDEN = -1e30


def kernel(
    span_ref, q_hbm, k_hbm, v_hbm, w_hbm, o_ref,
    qv, kw, vw, w_own, w_oth, acc, top, att, att_oth, pb, own, keep, relay, comb, final,
    lsem, hs, hr, ws, wr, zs, zr, xs, xr,
):
    head = lax.axis_index("head")
    frame = lax.axis_index("frame")
    frames = lax.axis_size("frame")
    zh, x = head // NX, head % NX
    core = frame % 2
    step = 1 - 2 * core
    sib = (head, frame + step)
    far = (head, frame - step)
    over = (head, frame + 2 * step)
    under = (head, frame - 2 * step)
    last = frames - 1
    far_ok = (frame - step >= 0) & (frame - step <= last)
    over_ok = (frame + 2 * step >= 0) & (frame + 2 * step <= last)
    zpart = ((1 - zh) * NX + x, frame)
    znear = ((1 - zh) * NX + x, (frame + frames // 2) % frames)
    right = (zh * NX + (x + 1) % NX, frame)
    left = (zh * NX + (x + NX - 1) % NX, frame)

    def rows(i):
        return pl.ds(pl.multiple_of((core + i) % 2 * T, T), T)

    def local(src, dst, n):
        copy = pltpu.make_async_copy(src, dst, lsem.at[n])
        copy.start()
        return copy

    def remote(src, dst, send, recv, device):
        return pltpu.make_async_remote_copy(
            src_ref=src, dst_ref=dst, send_sem=send, recv_sem=recv, device_id=device, device_id_type=MESH
        )

    q_in = [local(q_hbm.at[rows(i), :], qv.at[i], i) for i in range(2)]
    kv_in = [local(k_hbm.at[rows(i), :], kw.at[3 + i], 2 + i) for i in range(2)]
    kv_in += [local(v_hbm.at[rows(i), :], vw.at[3 + i], 4 + i) for i in range(2)]

    barrier = pltpu.get_barrier_semaphore()

    def greet(device):
        pl.semaphore_signal(barrier, inc=1, device_id=device, device_id_type=MESH)

    for device in (sib, zpart, znear, right, left):
        greet(device)

    @pl.when(far_ok)
    def _():
        greet(far)
        greet(under)

    @pl.when(over_ok)
    def _():
        greet(over)

    pl.semaphore_wait(barrier, 5 + 2 * far_ok.astype(jnp.int32) + over_ok.astype(jnp.int32))

    def halo(i, slot, device):
        return [
            remote(src.at[rows(i), :], dst.at[slot], hs.at[n, slot], hr.at[n, slot], device)
            for n, (src, dst) in enumerate(((k_hbm, kw), (v_hbm, vw)))
        ]

    to_far = [halo(0, 2, far), halo(1, 1, far)]
    to_sib = [halo(1, 5, sib), halo(0, 6, sib)]
    to_over = halo(1, 0, over)
    forward = [
        remote(buf.at[2], buf.at[7], hs.at[n, 7], hr.at[n, 7], sib) for n, buf in enumerate((kw, vw))
    ]

    @pl.when(far_ok)
    def _():
        for copy in to_far[0]:
            copy.start()

    for pair in to_sib:
        for copy in pair:
            copy.start()

    mine = pl.ds(pl.multiple_of(core * HALF, HALF), HALF)

    def columns(group, d):
        return pl.ds(pl.multiple_of(group * (NX * G) + d * G, G), G)

    w_near = [
        remote(w_hbm.at[mine, columns(1 - zh, d)], w_oth.at[d, mine, :], ws.at[d], wr.at[d], znear) for d in range(NX)
    ]
    w_pass = remote(w_oth.at[:, mine, :], w_oth.at[:, mine, :], ws.at[NX], wr.at[NX], sib)
    for copy in w_near:
        copy.start()
    w_in = [local(w_hbm.at[:, columns(zh, d)], w_own.at[d], 6 + d) for d in range(NX)]

    for copy in q_in + kv_in:
        copy.wait()

    def attend(i, hd, slots, first=False):
        cols = slice(hd * HD, (hd + 1) * HD)
        n = len(slots)
        query = qv[i, :, cols]
        keys = kw[slots[0] : slots[0] + n, :, cols].reshape(n * T, HD)
        values = vw[slots[0] : slots[0] + n, :, cols].reshape(n * T, HD)
        s = lax.dot_general(query, keys, (((1,), (1,)), ((), ())), preferred_element_type=F32) * SCALE
        span = span_ref[hd]
        bias = [jnp.where(jnp.abs(3 + i - slot) <= span, 0.0, HIDDEN).astype(F32) for slot in slots]
        new = None
        for b, part in zip(bias, [s[:, m * T : (m + 1) * T] for m in range(n)]):
            peak = jnp.max(part, axis=1, keepdims=True) + b
            new = peak if new is None else jnp.maximum(new, peak)
        new = jnp.broadcast_to(new, (T, HD))
        if not first:
            old = top[i, hd]
            new = jnp.maximum(old, new)
            shrink = jnp.exp2(old - new)
        shift = jnp.concatenate([new - b for b in bias for _ in range(T // HD)], axis=1)
        p = jnp.exp2(s - shift).astype(BF16)
        extended = jnp.concatenate([values, jnp.ones((n * T, HD), BF16)], axis=1)
        out = jnp.dot(p, extended, preferred_element_type=F32)
        top[i, hd] = new
        if first:
            acc[i, hd] = out
        else:
            acc[i, hd] = acc[i, hd] * jnp.concatenate([shrink, shrink], axis=1) + out

    def attend_both(slots, first=False):
        @pl.loop(0, 2)
        def _(i):
            for hd in range(NH):
                attend(i, hd, slots, first)

    def finish(i):
        for hd in range(NH):
            att[i, :, hd * HD : (hd + 1) * HD] = (acc[i, hd, :, :HD] / acc[i, hd, :, HD:]).astype(BF16)

    attend_both((3, 4), first=True)
    for pair in to_sib:
        for copy in pair:
            copy.wait_recv()
    attend_both((5, 6))

    @pl.when(far_ok)
    def _():
        for copy in to_far[0]:
            copy.wait_send()
        for copy in to_far[1]:
            copy.start()
        for copy in to_far[0]:
            copy.wait_recv()
        for copy in forward:
            copy.start()
        attend_both((2,))

    @pl.when(over_ok)
    def _():
        for copy in forward:
            copy.wait_recv()
        for hd in range(NH):
            attend(1, hd, (7,))

    @pl.when(far_ok)
    def _():
        for copy in to_far[1]:
            copy.wait_send()

    @pl.when(over_ok)
    def _():
        for copy in to_over:
            copy.start()

    @pl.when(far_ok)
    def _():
        for copy in to_far[1]:
            copy.wait_recv()
        attend_both((1,))

    to_z = [remote(att.at[i], att_oth.at[i], zs.at[i], zr.at[i], zpart) for i in range(2)]
    finish(1)
    to_z[1].start()
    for copy in w_near:
        copy.wait_recv()
    w_pass.start()
    for copy in w_in:
        copy.wait()

    @pl.when(far_ok)
    def _():
        for copy in to_over:
            copy.wait_recv()
        for hd in range(NH):
            attend(0, hd, (0,))

    finish(0)
    to_z[0].start()
    w_pass.wait_recv()

    lo, hi = pl.ds(0, HALF), pl.ds(HALF, HALF)

    def shift_x(i):
        def send(n, src, dst, device):
            return remote(src, dst, xs.at[i, n], xr.at[i, n], device)

        return [
            send(0, pb.at[i, 0, lo, :], relay.at[i, 0], right),
            send(1, pb.at[i, 0, hi, :], relay.at[i, 1], left),
            send(2, pb.at[i, 1, hi, :], final.at[i, 1], right),
            send(3, pb.at[i, 2, lo, :], final.at[i, 3], left),
            send(4, comb.at[i, 0], final.at[i, 0], right),
            send(5, comb.at[i, 1], final.at[i, 2], left),
        ]

    moves = [shift_x(i) for i in range(2)]

    def project(i):
        to_z[i].wait_recv()
        both = jnp.concatenate([att[i], att_oth[i]], axis=1)

        def block(r):
            d = (x + r) % NX
            return jnp.dot(both, jnp.concatenate([w_own[d], w_oth[d]], axis=0), preferred_element_type=F32)

        pb[i, 0] = block(2).astype(BF16)
        moves[i][0].start()
        moves[i][1].start()
        part = block(1)
        keep[i, 0] = part[:HALF]
        pb[i, 1, HALF:, :] = part[HALF:].astype(BF16)
        moves[i][2].start()
        part = block(3)
        keep[i, 1] = part[HALF:]
        pb[i, 2, :HALF, :] = part[:HALF].astype(BF16)
        moves[i][3].start()
        own[i] = block(0)

    def combine(i):
        for n in range(2):
            moves[i][n].wait_recv()
            comb[i, n] = (keep[i, n] + relay[i, n].astype(F32)).astype(BF16)
            moves[i][4 + n].start()

    def collect(i):
        for n in range(2, 6):
            moves[i][n].wait_recv()
        block = (core + i) % 2
        o_ref[block, :HALF, :] = (
            own[i, :HALF] + final[i, 0].astype(F32) + final[i, 3].astype(F32)
        ).astype(BF16)
        o_ref[block, HALF:, :] = (
            own[i, HALF:] + final[i, 1].astype(F32) + final[i, 2].astype(F32)
        ).astype(BF16)

    project(1)
    combine(1)
    project(0)
    combine(0)
    collect(1)
    collect(0)

    for pair in to_sib:
        for copy in pair:
            copy.wait_send()

    @pl.when(far_ok)
    def _():
        for copy in forward:
            copy.wait_send()

    @pl.when(over_ok)
    def _():
        for copy in to_over:
            copy.wait_send()

    for copy in w_near:
        copy.wait_send()
    w_pass.wait_send()
    for i in range(2):
        to_z[i].wait_send()
        for copy in moves[i]:
            copy.wait_send()


def body(query_tok, key_tok, value_tok, head_span, out_weight):
    anywhere = pl.BlockSpec(memory_space=pl.ANY)
    dma = pltpu.SemaphoreType.DMA
    out = pl.pallas_call(
        kernel,
        name="window_attention",
        out_shape=jax.ShapeDtypeStruct((2, T, G), BF16),
        in_specs=[pl.BlockSpec(memory_space=pltpu.SMEM)] + [anywhere] * 4,
        out_specs=pl.BlockSpec(memory_space=pltpu.VMEM),
        scratch_shapes=[
            pltpu.VMEM((2, T, G), BF16),
            pltpu.VMEM((8, T, G), BF16),
            pltpu.VMEM((8, T, G), BF16),
            pltpu.VMEM((NX, G, G), BF16),
            pltpu.VMEM((NX, G, G), BF16),
            pltpu.VMEM((2, NH, T, 2 * HD), F32),
            pltpu.VMEM((2, NH, T, HD), F32),
            pltpu.VMEM((2, T, G), BF16),
            pltpu.VMEM((2, T, G), BF16),
            pltpu.VMEM((2, 3, T, G), BF16),
            pltpu.VMEM((2, T, G), F32),
            pltpu.VMEM((2, 2, HALF, G), F32),
            pltpu.VMEM((2, 2, HALF, G), BF16),
            pltpu.VMEM((2, 2, HALF, G), BF16),
            pltpu.VMEM((2, 4, HALF, G), BF16),
            dma((10,)),
            dma((2, 8)),
            dma((2, 8)),
            dma((NX + 1,)),
            dma((NX + 1,)),
            dma((2,)),
            dma((2,)),
            dma((2, 6)),
            dma((2, 6)),
        ],
        compiler_params=pltpu.CompilerParams(
            collective_id=0, has_side_effects=True, vmem_limit_bytes=56 * 1024 * 1024
        ),
    )(head_span, query_tok, key_tok, value_tok, out_weight)
    return out.reshape(2 * T, G)


def solution(mesh):
    return jax.shard_map(
        body,
        mesh=mesh,
        in_specs=(
            P("frame", "head"),
            P("frame", "head"),
            P("frame", "head"),
            P("head"),
            P("head", None),
        ),
        out_specs=P("frame", "head"),
        check_vma=False,
    )
```

time: 229 us -> 62.1 us (0.27)
  the two profiles are of different devices: /device:TPU:24 before, /device:TPU:1 now
where the time goes in v1:
time: 62.1 us; the launch traced here: 61.9 us
  Pallas kernels  60 us (97%)
  local copies, waits for them, and re-layouts  1.94 us (3%)
    pallas_call x1, Pallas kernels, body(): pl.pallas_call(kernel, name='window_attention', out_shape=jax.ShapeDtypeS...  60 us
    unnamed x1, local copies, waits for them, and re-layouts  1.94 us

profile of v1, /device:TPU:1, one launch (start us, length us, event | category | flops | bytes accessed | tf_op | source)
XLA Modules:
  0.0 61.9 jit_solution(5508252335967407919)
XLA Ops:
  0.0 60.0 %window_attention.1 = bf16[2,384,384]{2,1,0:T(8,128)(2,1)} custom-call(s32[3]{0:T(128)} %span_ref.1, bf16[768,384]{1,0:T(8,128)(2,1)} %q_hbm.1, bf16[768,384]{1,0:T(8,128)(2,1)} %k_hbm.1, bf16[768,384]{1,0:T(8,128)(2,1)} %v_hbm.1, bf16[384,3072]{1,0:T(8,128)(2,1)} %w_hbm.1), custom_call_target="tpu_custom_call" | custom-call | tf_op jit(solution)/shard_map/window_attention/pallas_call | solution.py:308
  60.0 1.9 %copy.7 = bf16[768,384]{1,0:T(8,128)(2,1)} copy(bf16[768,384]{1,0:T(8,128)(2,1)} %bitcast.1) | data formatting | bytes 1179648

commit v2 on v0

v2 whole, which is shorter than its diff:
```python
import math

import jax
import jax.numpy as jnp
from jax import lax
from jax.experimental import pallas as pl
from jax.experimental.pallas import tpu as pltpu
from jax.sharding import PartitionSpec as P

MESH = pl.DeviceIdType.MESH
HD = 128
T = 384
HALF = T // 2
G = 384
NH = 3
NX = 4
F32 = jnp.float32
BF16 = jnp.bfloat16
SCALE = math.log2(math.e) / math.sqrt(HD)
HIDDEN = -1e30


def kernel(
    span_ref, q_hbm, k_hbm, v_hbm, w_hbm, o_ref,
    qv, kv, wb, acc, top, att, pz, own, got,
    lsem, hs, hr, es, er, ws, wr, xs, xr, rs, rr, zs, zr,
):
    head = lax.axis_index("head")
    frame = lax.axis_index("frame")
    frames = lax.axis_size("frame")
    zh, x = head // NX, head % NX
    core = frame % 2
    step = 1 - 2 * core
    sib = (head, frame + step)
    far = (head, frame - step)
    over = (head, frame + 2 * step)
    under = (head, frame - 2 * step)
    last = frames - 1
    far_ok = (frame - step >= 0) & (frame - step <= last)
    over_ok = (frame + 2 * step >= 0) & (frame + 2 * step <= last)
    zpart = ((1 - zh) * NX + x, frame)
    right = (zh * NX + (x + 1) % NX, frame)
    left = (zh * NX + (x + NX - 1) % NX, frame)
    across = (zh * NX + (x + 2) % NX, frame)

    def rows(i):
        return pl.ds(pl.multiple_of((core + i) % 2 * T, T), T)

    def columns(g, d):
        group = zh if g else 1 - zh
        return pl.ds(pl.multiple_of((group * NX + d) * G, G), G)

    def local(src, dst, n):
        copy = pltpu.make_async_copy(src, dst, lsem.at[n])
        copy.start()
        return copy

    def remote(src, dst, send, recv, device):
        return pltpu.make_async_remote_copy(
            src_ref=src, dst_ref=dst, send_sem=send, recv_sem=recv, device_id=device, device_id_type=MESH
        )

    own_in, n = [], 0
    for i in range(2):
        for hd in range(NH):
            cols = pl.ds(hd * HD, HD)
            own_in.append(local(k_hbm.at[rows(i), cols], kv.at[3 + i, hd, 0], n))
            own_in.append(local(v_hbm.at[rows(i), cols], kv.at[3 + i, hd, 1], n + 1))
            own_in.append(local(q_hbm.at[rows(i), cols], qv.at[i, hd], n + 2))
            n += 3
    w_in = [local(w_hbm.at[:, columns(g, x)], wb.at[g, 0], n + g) for g in range(2)]

    barrier = pltpu.get_barrier_semaphore()

    def greet(device):
        pl.semaphore_signal(barrier, inc=1, device_id=device, device_id_type=MESH)

    for device in (sib, zpart, right, left, across):
        greet(device)

    @pl.when(far_ok)
    def _():
        greet(far)
        greet(under)

    @pl.when(over_ok)
    def _():
        greet(over)

    for copy in own_in:
        copy.wait()
    pl.semaphore_wait(barrier, 5 + 2 * far_ok.astype(jnp.int32) + over_ok.astype(jnp.int32))

    def halo(src, dst, device, hd):
        return remote(kv.at[src, hd], kv.at[dst, hd], hs.at[dst, hd], hr.at[dst, hd], device)

    def to_far(hd):
        return halo(3, 2, far, hd)

    def to_sib(src, hd):
        return halo(src, 9 - src, sib, hd)

    def to_over(hd):
        return halo(5, 1, over, hd)

    def forward(hd):
        return halo(2, 7, sib, hd)

    def edge_keys(hd):
        return remote(kv.at[4, hd, 0], kv.at[0, hd, 0], es.at[0, hd], er.at[0, hd], over)

    def edge_values(hd):
        return remote(kv.at[5, hd, 1], kv.at[0, hd, 1], es.at[1, hd], er.at[1, hd], far)

    def each(*actions):
        @pl.loop(0, NH)
        def _(hd):
            for action in actions:
                action(hd)

    @pl.when(far_ok)
    def _():
        each(lambda hd: to_far(hd).start())

    each(lambda hd: to_sib(4, hd).start())
    each(lambda hd: to_sib(3, hd).start())

    mine = pl.ds(pl.multiple_of(core * HALF, HALF), HALF)
    w_out = [
        remote(w_hbm.at[mine, columns(g, (x + r) % NX)], wb.at[g, NX - r, mine, :], ws.at[r - 1, g], wr.at[r - 1, g], device)
        for r, device in ((2, across), (1, right), (3, left))
        for g in range(2)
    ]
    w_pass = [
        remote(wb.at[:, r, mine, :], wb.at[:, r, mine, :], ws.at[NX - 2 + r, 0], wr.at[NX - 2 + r, 0], sib)
        for r in range(1, NX)
    ]
    for copy in w_out:
        copy.start()

    def attend(i, hd, slot, n, first=False):
        keys = kv[slot : slot + n, hd, 0].reshape(n * T, HD)
        values = kv[slot : slot + n, hd, 1].reshape(n * T, HD)
        s = lax.dot_general(qv[i, hd], keys, (((1,), (1,)), ((), ())), preferred_element_type=F32) * SCALE
        span = span_ref[hd]
        bias = [jnp.where(jnp.abs(3 + i - slot - m) <= span, 0.0, HIDDEN).astype(F32) for m in range(n)]
        new = None
        for m in range(n):
            peak = jnp.max(s[:, m * T : (m + 1) * T], axis=1, keepdims=True) + bias[m]
            new = peak if new is None else jnp.maximum(new, peak)
        new = jnp.broadcast_to(new, (T, HD))
        if not first:
            old = top[i, hd]
            new = jnp.maximum(old, new)
            shrink = jnp.exp2(old - new)
        shift = jnp.concatenate([new - b for b in bias for _ in range(T // HD)], axis=1)
        p = jnp.exp2(s - shift).astype(BF16)
        extended = jnp.concatenate([values, jnp.ones((n * T, HD), BF16)], axis=1)
        out = jnp.dot(p, extended, preferred_element_type=F32)
        top[i, hd] = new
        if first:
            acc[i, hd] = out
        else:
            acc[i, hd] = acc[i, hd] * jnp.concatenate([shrink, shrink], axis=1) + out

    def attend_both(slot, n, first=False):
        @pl.loop(0, 2 * NH)
        def _(u):
            attend(u // NH, u % NH, slot, n, first)

    def to_right(i, hd):
        return remote(att.at[i, 0, hd], att.at[i, 3, hd], xs.at[i, 0, hd], xr.at[i, 0, hd], right)

    def to_left(i, hd):
        return remote(att.at[i, 0, hd], att.at[i, 1, hd], xs.at[i, 1, hd], xr.at[i, 1, hd], left)

    def onward_right(i, hd):
        part = pl.ds(0, HALF)
        return remote(att.at[i, 3, hd, part], att.at[i, 2, hd, part], rs.at[i, 0, hd], rr.at[i, 0, hd], right)

    def onward_left(i, hd):
        part = pl.ds(HALF, HALF)
        return remote(att.at[i, 1, hd, part], att.at[i, 2, hd, part], rs.at[i, 1, hd], rr.at[i, 1, hd], left)

    def finish(i, hd):
        att[i, 0, hd] = (acc[i, hd, :, :HD] / acc[i, hd, :, HD:]).astype(BF16)
        to_right(i, hd).start()
        to_left(i, hd).start()

    def pass_on(i, hd):
        to_right(i, hd).wait_recv()
        onward_right(i, hd).start()
        to_left(i, hd).wait_recv()
        onward_left(i, hd).start()

    def to_z(i):
        return remote(pz.at[i], got.at[i], zs.at[i], zr.at[i], zpart)

    def project(i):
        each(lambda hd: onward_right(i, hd).wait_recv(), lambda hd: onward_left(i, hd).wait_recv())
        rows_of = jnp.concatenate([att[i, r, hd] for r in range(NX) for hd in range(NH)], axis=1)

        def block(g):
            weight = jnp.concatenate([wb[g, r] for r in range(NX)], axis=0)
            return jnp.dot(rows_of, weight, preferred_element_type=F32)

        pz[i] = block(0).astype(BF16)
        to_z(i).start()
        own[i] = block(1)

    def collect(i):
        to_z(i).wait_recv()
        o_ref[(core + i) % 2] = (own[i] + got[i].astype(F32)).astype(BF16)

    attend_both(3, 2, first=True)
    each(lambda hd: to_sib(4, hd).wait_recv())

    @pl.when(over_ok)
    def _():
        each(lambda hd: to_over(hd).start())

    each(lambda hd: to_sib(3, hd).wait_recv())
    attend_both(5, 2)

    @pl.when(far_ok)
    def _():
        each(lambda hd: to_far(hd).wait_recv(), lambda hd: forward(hd).start())
        each(lambda hd: to_far(hd).wait_send(), lambda hd: edge_values(hd).start())

    @pl.when(over_ok)
    def _():
        each(lambda hd: to_over(hd).wait_send(), lambda hd: edge_keys(hd).start())

    @pl.loop(0, NH)
    def _(hd):
        @pl.when(far_ok)
        def _():
            to_over(hd).wait_recv()
            attend(1, hd, 1, 2)

        @pl.when(over_ok)
        def _():
            forward(hd).wait_recv()
            attend(1, hd, 7, 1)

        finish(1, hd)

    for copy in w_out:
        copy.wait_recv()
    for copy in w_pass:
        copy.start()

    @pl.loop(0, NH)
    def _(hd):
        @pl.when(far_ok)
        def _():
            attend(0, hd, 1, 2)

        pass_on(1, hd)

    @pl.loop(0, NH)
    def _(hd):
        @pl.when(far_ok)
        def _():
            edge_keys(hd).wait_recv()
            edge_values(hd).wait_recv()
            attend(0, hd, 0, 1)

        finish(0, hd)

    for copy in w_in:
        copy.wait()
    for copy in w_pass:
        copy.wait_recv()
    project(1)
    each(lambda hd: pass_on(0, hd))
    project(0)
    collect(1)
    collect(0)

    each(lambda hd: to_sib(4, hd).wait_send(), lambda hd: to_sib(3, hd).wait_send())

    @pl.when(far_ok)
    def _():
        each(lambda hd: forward(hd).wait_send(), lambda hd: edge_values(hd).wait_send())

    @pl.when(over_ok)
    def _():
        each(lambda hd: edge_keys(hd).wait_send())

    for copy in w_out + w_pass:
        copy.wait_send()
    for i in range(2):
        each(
            lambda hd: to_right(i, hd).wait_send(),
            lambda hd: to_left(i, hd).wait_send(),
            lambda hd: onward_right(i, hd).wait_send(),
            lambda hd: onward_left(i, hd).wait_send(),
        )
        to_z(i).wait_send()


def body(query_tok, key_tok, value_tok, head_span, out_weight):
    anywhere = pl.BlockSpec(memory_space=pl.ANY)
    dma = pltpu.SemaphoreType.DMA
    out = pl.pallas_call(
        kernel,
        name="window_attention",
        out_shape=pltpu.VMEM((2, T, G), BF16),
        in_specs=[pl.BlockSpec(memory_space=pltpu.SMEM)] + [anywhere] * 4,
        out_specs=pl.BlockSpec(memory_space=pltpu.VMEM),
        scratch_shapes=[
            pltpu.VMEM((2, NH, T, HD), BF16),
            pltpu.VMEM((8, NH, 2, T, HD), BF16),
            pltpu.VMEM((2, NX, G, G), BF16),
            pltpu.VMEM((2, NH, T, 2 * HD), F32),
            pltpu.VMEM((2, NH, T, HD), F32),
            pltpu.VMEM((2, NX, NH, T, HD), BF16),
            pltpu.VMEM((2, T, G), BF16),
            pltpu.VMEM((2, T, G), F32),
            pltpu.VMEM((2, T, G), BF16),
            dma((20,)),
            dma((8, NH)),
            dma((8, NH)),
            dma((2, NH)),
            dma((2, NH)),
            dma((6, 2)),
            dma((6, 2)),
            dma((2, 2, NH)),
            dma((2, 2, NH)),
            dma((2, 2, NH)),
            dma((2, 2, NH)),
            dma((2,)),
            dma((2,)),
        ],
        compiler_params=pltpu.CompilerParams(
            collective_id=0, has_side_effects=True, vmem_limit_bytes=56 * 1024 * 1024
        ),
    )(head_span, query_tok, key_tok, value_tok, out_weight)
    return out.reshape(2 * T, G)


def solution(mesh):
    return jax.shard_map(
        body,
        mesh=mesh,
        in_specs=(
            P("frame", "head"),
            P("frame", "head"),
            P("frame", "head"),
            P("head"),
            P("head", None),
        ),
        out_specs=P("frame", "head"),
        check_vma=False,
    )
```

time: 229 us -> 56.3 us (0.25)
  waiting for transfers between devices: 97 us -> 0 us
  Pallas kernels: 0 us -> 54.6 us
  local copies, waits for them, and re-layouts: 43.4 us -> 0.82 us
  matrix products: 31.3 us -> 0 us
  starting transfers between devices: 24.6 us -> 0 us
  other arithmetic: 17.3 us -> 0 us
  between operations: 13.6 us -> 0.01 us
    unnamed x2 -> x0, waiting for transfers between devices: 91.9 us -> none
    pallas_call x0 -> x1, Pallas kernels: none -> 54.6 us  [body(): pl.pallas_call(kernel, name='window_attention', out_shape=pltpu.VMEM((2,...]
    reshape x6 -> x0, local copies, waits for them, and re-layouts: 24.7 us -> none  [the longest x2 10.1 us: body(): value_window[local:local + 7].reshape(7 * FRAME_TOK, heads_here, HD)]
    ppermute x8 -> x0, starting transfers between devices: 24.6 us -> none  [from_behind(): lax.ppermute(value, axis, [(source, source + steps) for source in range(l...]
    sub x2 -> x0, matrix products: 17.5 us -> none  [attend_frame(): weights = jnp.where(visible, jnp.exp(scores - rowmax), 0.0)]
    concatenate x3 -> x0, other arithmetic: 16.5 us -> none  [the longest x1 8.41 us: body(): jnp.concatenate([lower[0], received[1][0], key_local, received[-1][0], up...]
    dot_general x3 -> x0, matrix products: 13.8 us -> none  [the longest x2 9.4 us: attend_frame(): jnp.einsum('hqk,khd->qhd', probs, value_rows, preferred_element_type=jnp....]
    unnamed x16 -> x1, local copies, waits for them, and re-layouts: 13.3 us -> 0.82 us
  transfers between devices with their start and end apart: 9 -> 0, of which waited for: 3 -> 0; matrix products, arithmetic and copies ran while one was open for 12% -> 0% of each run, Pallas kernels for 0% -> 0%
where the time goes in v2:
time: 56.3 us; the launch traced here: 55.4 us
  Pallas kernels  54.6 us (97%)
  local copies, waits for them, and re-layouts  0.82 us (1%)
    pallas_call x1, Pallas kernels, body(): pl.pallas_call(kernel, name='window_attention', out_shape=pltpu.VMEM((2,...  54.6 us

profile of v2, /device:TPU:24, one launch (start us, length us, event | category | flops | bytes accessed | tf_op | source)
XLA Modules:
  0.0 55.4 jit_solution(14278144415592608348)
XLA Ops:
  0.0 54.6 %window_attention.1 = bf16[2,384,384]{2,1,0:T(8,128)(2,1)S(1)} custom-call(s32[3]{0:T(128)} %span_ref.1, bf16[768,384]{1,0:T(8,128)(2,1)} %q_hbm.1, bf16[768,384]{1,0:T(8,128)(2,1)} %k_hbm.1, bf16[768,384]{1,0:T(8,128)(2,1)} %v_hbm.1, bf16[384,3072]{1,0:T(8,128)(2,1)} %w_hbm.1), custom_call_target="tpu_custom_call" | custom-call | tf_op jit(solution)/shard_map/window_attention/pallas_call | solution.py:306
  54.6 0.8 %copy.7 = bf16[768,384]{1,0:T(8,128)(2,1)} copy(bf16[768,384]{1,0:T(8,128)(2,1)S(1)} %bitcast.1) | data formatting | bytes 1179648

commit v3 on v2

--- a/solution.py
+++ b/solution.py
@@ -22,7 +22,7 @@
 
 def kernel(
     span_ref, q_hbm, k_hbm, v_hbm, w_hbm, o_ref,
-    qv, kv, wb, acc, top, att, pz, own, got,
+    qv, kv, wb, acc, top, att, pz, part, got,
     lsem, hs, hr, es, er, ws, wr, xs, xr, rs, rr, zs, zr,
 ):
     head = lax.axis_index("head")
@@ -120,10 +120,9 @@
 
     @pl.when(far_ok)
     def _():
-        each(lambda hd: to_far(hd).start())
-
-    each(lambda hd: to_sib(4, hd).start())
-    each(lambda hd: to_sib(3, hd).start())
+        to_far(0).start()
+
+    each(lambda hd: to_sib(4, hd).start(), lambda hd: to_sib(3, hd).start())
 
     mine = pl.ds(pl.multiple_of(core * HALF, HALF), HALF)
     w_out = [
@@ -163,87 +162,114 @@
         else:
             acc[i, hd] = acc[i, hd] * jnp.concatenate([shrink, shrink], axis=1) + out
 
-    def attend_both(slot, n, first=False):
-        @pl.loop(0, 2 * NH)
-        def _(u):
-            attend(u // NH, u % NH, slot, n, first)
-
-    def to_right(i, hd):
-        return remote(att.at[i, 0, hd], att.at[i, 3, hd], xs.at[i, 0, hd], xr.at[i, 0, hd], right)
-
-    def to_left(i, hd):
-        return remote(att.at[i, 0, hd], att.at[i, 1, hd], xs.at[i, 1, hd], xr.at[i, 1, hd], left)
-
-    def onward_right(i, hd):
-        part = pl.ds(0, HALF)
-        return remote(att.at[i, 3, hd, part], att.at[i, 2, hd, part], rs.at[i, 0, hd], rr.at[i, 0, hd], right)
-
-    def onward_left(i, hd):
-        part = pl.ds(HALF, HALF)
-        return remote(att.at[i, 1, hd, part], att.at[i, 2, hd, part], rs.at[i, 1, hd], rr.at[i, 1, hd], left)
+    def piece(i, source, k, part=None):
+        if i:
+            ref = att.at[i, source, k]
+            return ref if part is None else ref.at[pl.ds(part * HALF, HALF)]
+        if part is None:
+            return att.at[i, source, :, pl.ds(k * HALF, HALF)]
+        return att.at[i, source, :, pl.ds(k * HALF + part * (HALF // 2), HALF // 2)]
+
+    def to_right(i, k):
+        return remote(piece(i, 0, k), piece(i, 3, k), xs.at[i, 0, k], xr.at[i, 0, k], right)
+
+    def to_left(i, k):
+        return remote(piece(i, 0, k), piece(i, 1, k), xs.at[i, 1, k], xr.at[i, 1, k], left)
+
+    def onward_right(i, k):
+        return remote(piece(i, 3, k, 0), piece(i, 2, k, 0), rs.at[i, 0, k], rr.at[i, 0, k], right)
+
+    def onward_left(i, k):
+        return remote(piece(i, 1, k, 1), piece(i, 2, k, 1), rs.at[i, 1, k], rr.at[i, 1, k], left)
 
     def finish(i, hd):
         att[i, 0, hd] = (acc[i, hd, :, :HD] / acc[i, hd, :, HD:]).astype(BF16)
-        to_right(i, hd).start()
-        to_left(i, hd).start()
-
-    def pass_on(i, hd):
-        to_right(i, hd).wait_recv()
-        onward_right(i, hd).start()
-        to_left(i, hd).wait_recv()
-        onward_left(i, hd).start()
-
-    def to_z(i):
-        return remote(pz.at[i], got.at[i], zs.at[i], zr.at[i], zpart)
-
-    def project(i):
-        each(lambda hd: onward_right(i, hd).wait_recv(), lambda hd: onward_left(i, hd).wait_recv())
-        rows_of = jnp.concatenate([att[i, r, hd] for r in range(NX) for hd in range(NH)], axis=1)
-
-        def block(g):
+
+    def send_x(i, k):
+        to_right(i, k).start()
+        to_left(i, k).start()
+
+    def pass_on(i, k):
+        to_right(i, k).wait_recv()
+        onward_right(i, k).start()
+        to_left(i, k).wait_recv()
+        onward_left(i, k).start()
+
+    def gathered_x(i, k):
+        onward_right(i, k).wait_recv()
+        onward_left(i, k).wait_recv()
+
+    def to_z(i, k, size):
+        where = pl.ds(k * size, size)
+        return remote(pz.at[i, where], got.at[i, where], zs.at[2 * i + k], zr.at[2 * i + k], zpart)
+
+    def project(i, k, size):
+        where = slice(k * size, (k + 1) * size)
+        gathered = jnp.concatenate([att[i, r, hd, where] for r in range(NX) for hd in range(NH)], axis=1)
+
+        def columns_of(g):
             weight = jnp.concatenate([wb[g, r] for r in range(NX)], axis=0)
-            return jnp.dot(rows_of, weight, preferred_element_type=F32)
-
-        pz[i] = block(0).astype(BF16)
-        to_z(i).start()
-        own[i] = block(1)
-
-    def collect(i):
-        to_z(i).wait_recv()
-        o_ref[(core + i) % 2] = (own[i] + got[i].astype(F32)).astype(BF16)
-
-    attend_both(3, 2, first=True)
-    each(lambda hd: to_sib(4, hd).wait_recv())
-
-    @pl.when(over_ok)
-    def _():
-        each(lambda hd: to_over(hd).start())
-
-    each(lambda hd: to_sib(3, hd).wait_recv())
-    attend_both(5, 2)
-
-    @pl.when(far_ok)
-    def _():
-        each(lambda hd: to_far(hd).wait_recv(), lambda hd: forward(hd).start())
-        each(lambda hd: to_far(hd).wait_send(), lambda hd: edge_values(hd).start())
-
-    @pl.when(over_ok)
-    def _():
-        each(lambda hd: to_over(hd).wait_send(), lambda hd: edge_keys(hd).start())
-
-    @pl.loop(0, NH)
-    def _(hd):
-        @pl.when(far_ok)
-        def _():
-            to_over(hd).wait_recv()
-            attend(1, hd, 1, 2)
-
-        @pl.when(over_ok)
-        def _():
-            forward(hd).wait_recv()
-            attend(1, hd, 7, 1)
-
-        finish(1, hd)
+            return jnp.dot(gathered, weight, preferred_element_type=F32)
+
+        pz[i, where] = columns_of(0).astype(BF16)
+        to_z(i, k, size).start()
+        part[i, where] = columns_of(1)
+
+    def collect(i, k, size):
+        to_z(i, k, size).wait_recv()
+        where = slice(k * size, (k + 1) * size)
+        o_ref[(core + i) % 2, where] = (part[i, where] + got[i, where].astype(F32)).astype(BF16)
+
+    @pl.loop(0, NH + 1)
+    def _(step_no):
+        hd = step_no
+        before = step_no - 1
+
+        @pl.when(far_ok & (step_no > 0))
+        def _():
+            to_far(before).wait_recv()
+            forward(before).start()
+
+        @pl.when(step_no < NH)
+        def _():
+            to_sib(4, hd).wait_recv()
+
+            @pl.when(over_ok)
+            def _():
+                to_over(hd).start()
+
+            @pl.when(far_ok & (hd < NH - 1))
+            def _():
+                to_far(hd + 1).start()
+
+            to_sib(3, hd).wait_recv()
+            for i in range(2):
+                attend(i, hd, 3, 4, first=True)
+
+        @pl.when(step_no == NH - 1)
+        def _():
+            @pl.when(far_ok)
+            def _():
+                each(lambda hd: edge_values(hd).start())
+
+            @pl.when(over_ok)
+            def _():
+                each(lambda hd: edge_keys(hd).start())
+
+        @pl.when(step_no > 0)
+        def _():
+            @pl.when(far_ok)
+            def _():
+                to_over(before).wait_recv()
+                attend(1, before, 1, 2)
+
+            @pl.when(over_ok)
+            def _():
+                forward(before).wait_recv()
+                attend(1, before, 7, 1)
+
+            finish(1, before)
+            send_x(1, before)
 
     for copy in w_out:
         copy.wait_recv()
@@ -268,36 +294,46 @@
 
         finish(0, hd)
 
+    send_x(0, 0)
+    send_x(0, 1)
     for copy in w_in:
         copy.wait()
     for copy in w_pass:
         copy.wait_recv()
-    project(1)
-    each(lambda hd: pass_on(0, hd))
-    project(0)
-    collect(1)
-    collect(0)
+    each(lambda hd: gathered_x(1, hd))
+    project(1, 0, T)
+    pass_on(0, 0)
+    pass_on(0, 1)
+    for k in range(2):
+        gathered_x(0, k)
+        project(0, k, HALF)
+    collect(1, 0, T)
+    for k in range(2):
+        collect(0, k, HALF)
 
     each(lambda hd: to_sib(4, hd).wait_send(), lambda hd: to_sib(3, hd).wait_send())
 
     @pl.when(far_ok)
     def _():
-        each(lambda hd: forward(hd).wait_send(), lambda hd: edge_values(hd).wait_send())
+        each(
+            lambda hd: to_far(hd).wait_send(),
+            lambda hd: forward(hd).wait_send(),
+            lambda hd: edge_values(hd).wait_send(),
+        )
 
     @pl.when(over_ok)
     def _():
-        each(lambda hd: edge_keys(hd).wait_send())
+        each(lambda hd: to_over(hd).wait_send(), lambda hd: edge_keys(hd).wait_send())
 
     for copy in w_out + w_pass:
         copy.wait_send()
-    for i in range(2):
-        each(
-            lambda hd: to_right(i, hd).wait_send(),
-            lambda hd: to_left(i, hd).wait_send(),
-            lambda hd: onward_right(i, hd).wait_send(),
-            lambda hd: onward_left(i, hd).wait_send(),
-        )
-        to_z(i).wait_send()
+    for i, pieces in ((1, NH), (0, 2)):
+        for k in range(pieces):
+            for move in (to_right, to_left, onward_right, onward_left):
+                move(i, k).wait_send()
+    to_z(1, 0, T).wait_send()
+    for k in range(2):
+        to_z(0, k, HALF).wait_send()
 
 
 def body(query_tok, key_tok, value_tok, head_span, out_weight):
@@ -330,8 +366,8 @@
             dma((2, 2, NH)),
             dma((2, 2, NH)),
             dma((2, 2, NH)),
-            dma((2,)),
-            dma((2,)),
+            dma((3,)),
+            dma((3,)),
         ],
         compiler_params=pltpu.CompilerParams(
             collective_id=0, has_side_effects=True, vmem_limit_bytes=56 * 1024 * 1024

time: 56.3 us -> 52 us (0.924); the launches traced: 55.4 us -> 51.7 us
  Pallas kernels: 54.6 us -> 50.9 us
    pallas_call x1, Pallas kernels: 54.6 us -> 50.9 us  [body(): pl.pallas_call(kernel, name='window_attention', out_shape=pltpu.VMEM((2,...]
where the time goes in v3:
time: 52 us; the launch traced here: 51.7 us
  Pallas kernels  50.9 us (98%)
  local copies, waits for them, and re-layouts  0.82 us (2%)
    pallas_call x1, Pallas kernels, body(): pl.pallas_call(kernel, name='window_attention', out_shape=pltpu.VMEM((2,...  50.9 us

profile of v3, /device:TPU:24, one launch (start us, length us, event | category | flops | bytes accessed | tf_op | source)
XLA Modules:
  0.0 51.7 jit_solution(14266358748491635301)
XLA Ops:
  0.0 50.9 %window_attention.1 = bf16[2,384,384]{2,1,0:T(8,128)(2,1)S(1)} custom-call(s32[3]{0:T(128)} %span_ref.1, bf16[768,384]{1,0:T(8,128)(2,1)} %q_hbm.1, bf16[768,384]{1,0:T(8,128)(2,1)} %k_hbm.1, bf16[768,384]{1,0:T(8,128)(2,1)} %v_hbm.1, bf16[384,3072]{1,0:T(8,128)(2,1)} %w_hbm.1), custom_call_target="tpu_custom_call" | custom-call | tf_op jit(solution)/shard_map/window_attention/pallas_call | solution.py:342
  50.9 0.8 %copy.7 = bf16[768,384]{1,0:T(8,128)(2,1)} copy(bf16[768,384]{1,0:T(8,128)(2,1)S(1)} %bitcast.1) | data formatting | bytes 1179648

commit v4 on v3

--- a/solution.py
+++ b/solution.py
@@ -11,6 +11,8 @@
 HD = 128
 T = 384
 HALF = T // 2
+PIECES = 3
+PIECE = T // PIECES
 G = 384
 NH = 3
 NX = 4
@@ -60,6 +62,23 @@
             src_ref=src, dst_ref=dst, send_sem=send, recv_sem=recv, device_id=device, device_id_type=MESH
         )
 
+    barrier = pltpu.get_barrier_semaphore()
+
+    def greet(device):
+        pl.semaphore_signal(barrier, inc=1, device_id=device, device_id_type=MESH)
+
+    for device in (sib, zpart, right, left, across):
+        greet(device)
+
+    @pl.when(far_ok)
+    def _():
+        greet(far)
+        greet(under)
+
+    @pl.when(over_ok)
+    def _():
+        greet(over)
+
     own_in, n = [], 0
     for i in range(2):
         for hd in range(NH):
@@ -69,23 +88,6 @@
             own_in.append(local(q_hbm.at[rows(i), cols], qv.at[i, hd], n + 2))
             n += 3
     w_in = [local(w_hbm.at[:, columns(g, x)], wb.at[g, 0], n + g) for g in range(2)]
-
-    barrier = pltpu.get_barrier_semaphore()
-
-    def greet(device):
-        pl.semaphore_signal(barrier, inc=1, device_id=device, device_id_type=MESH)
-
-    for device in (sib, zpart, right, left, across):
-        greet(device)
-
-    @pl.when(far_ok)
-    def _():
-        greet(far)
-        greet(under)
-
-    @pl.when(over_ok)
-    def _():
-        greet(over)
 
     for copy in own_in:
         copy.wait()
@@ -167,8 +169,8 @@
             ref = att.at[i, source, k]
             return ref if part is None else ref.at[pl.ds(part * HALF, HALF)]
         if part is None:
-            return att.at[i, source, :, pl.ds(k * HALF, HALF)]
-        return att.at[i, source, :, pl.ds(k * HALF + part * (HALF // 2), HALF // 2)]
+            return att.at[i, source, :, pl.ds(k * PIECE, PIECE)]
+        return att.at[i, source, :, pl.ds(k * PIECE + part * (PIECE // 2), PIECE // 2)]
 
     def to_right(i, k):
         return remote(piece(i, 0, k), piece(i, 3, k), xs.at[i, 0, k], xr.at[i, 0, k], right)
@@ -201,7 +203,7 @@
 
     def to_z(i, k, size):
         where = pl.ds(k * size, size)
-        return remote(pz.at[i, where], got.at[i, where], zs.at[2 * i + k], zr.at[2 * i + k], zpart)
+        return remote(pz.at[i, where], got.at[i, where], zs.at[PIECES * i + k], zr.at[PIECES * i + k], zpart)
 
     def project(i, k, size):
         where = slice(k * size, (k + 1) * size)
@@ -246,7 +248,7 @@
             for i in range(2):
                 attend(i, hd, 3, 4, first=True)
 
-        @pl.when(step_no == NH - 1)
+        @pl.when(step_no == NH)
         def _():
             @pl.when(far_ok)
             def _():
@@ -255,6 +257,10 @@
             @pl.when(over_ok)
             def _():
                 each(lambda hd: edge_keys(hd).start())
+
+        @pl.when(step_no == NH)
+        def _():
+            pass_on(1, 0)
 
         @pl.when(step_no > 0)
         def _():
@@ -271,45 +277,44 @@
             finish(1, before)
             send_x(1, before)
 
+    pass_on(1, 1)
     for copy in w_out:
         copy.wait_recv()
     for copy in w_pass:
         copy.start()
 
-    @pl.loop(0, NH)
-    def _(hd):
-        @pl.when(far_ok)
-        def _():
+    @pl.when(far_ok)
+    def _():
+        for hd in range(NH):
             attend(0, hd, 1, 2)
 
-        pass_on(1, hd)
-
-    @pl.loop(0, NH)
-    def _(hd):
-        @pl.when(far_ok)
-        def _():
-            edge_keys(hd).wait_recv()
-            edge_values(hd).wait_recv()
+    pass_on(1, NH - 1)
+
+    @pl.when(far_ok)
+    def _():
+        each(lambda hd: edge_keys(hd).wait_recv(), lambda hd: edge_values(hd).wait_recv())
+        for hd in range(NH):
             attend(0, hd, 0, 1)
 
+    for hd in range(NH):
         finish(0, hd)
 
-    send_x(0, 0)
-    send_x(0, 1)
+    for k in range(PIECES):
+        send_x(0, k)
     for copy in w_in:
         copy.wait()
     for copy in w_pass:
         copy.wait_recv()
     each(lambda hd: gathered_x(1, hd))
     project(1, 0, T)
-    pass_on(0, 0)
-    pass_on(0, 1)
-    for k in range(2):
+    for k in range(PIECES):
+        pass_on(0, k)
+    for k in range(PIECES):
         gathered_x(0, k)
-        project(0, k, HALF)
+        project(0, k, PIECE)
     collect(1, 0, T)
-    for k in range(2):
-        collect(0, k, HALF)
+    for k in range(PIECES):
+        collect(0, k, PIECE)
 
     each(lambda hd: to_sib(4, hd).wait_send(), lambda hd: to_sib(3, hd).wait_send())
 
@@ -327,13 +332,13 @@
 
     for copy in w_out + w_pass:
         copy.wait_send()
-    for i, pieces in ((1, NH), (0, 2)):
+    for i, pieces in ((1, NH), (0, PIECES)):
         for k in range(pieces):
             for move in (to_right, to_left, onward_right, onward_left):
                 move(i, k).wait_send()
     to_z(1, 0, T).wait_send()
-    for k in range(2):
-        to_z(0, k, HALF).wait_send()
+    for k in range(PIECES):
+        to_z(0, k, PIECE).wait_send()
 
 
 def body(query_tok, key_tok, value_tok, head_span, out_weight):
@@ -366,8 +371,8 @@
             dma((2, 2, NH)),
             dma((2, 2, NH)),
             dma((2, 2, NH)),
-            dma((3,)),
-            dma((3,)),
+            dma((PIECES + 1,)),
+            dma((PIECES + 1,)),
         ],
         compiler_params=pltpu.CompilerParams(
             collective_id=0, has_side_effects=True, vmem_limit_bytes=56 * 1024 * 1024

time: 52 us -> 51.1 us (0.983)
  Pallas kernels: 50.9 us -> 50.1 us
    pallas_call x1, Pallas kernels: 50.9 us -> 50.1 us  [body(): pl.pallas_call(kernel, name='window_attention', out_shape=pltpu.VMEM((2,...]
where the time goes in v4:
time: 51.1 us; the launch traced here: 50.9 us
  Pallas kernels  50.1 us (98%)
  local copies, waits for them, and re-layouts  0.82 us (2%)
    pallas_call x1, Pallas kernels, body(): pl.pallas_call(kernel, name='window_attention', out_shape=pltpu.VMEM((2,...  50.1 us

profile of v4, /device:TPU:24, one launch (start us, length us, event | category | flops | bytes accessed | tf_op | source)
XLA Modules:
  0.0 50.9 jit_solution(13342238146249767751)
XLA Ops:
  0.0 50.1 %window_attention.1 = bf16[2,384,384]{2,1,0:T(8,128)(2,1)S(1)} custom-call(s32[3]{0:T(128)} %span_ref.1, bf16[768,384]{1,0:T(8,128)(2,1)} %q_hbm.1, bf16[768,384]{1,0:T(8,128)(2,1)} %k_hbm.1, bf16[768,384]{1,0:T(8,128)(2,1)} %v_hbm.1, bf16[384,3072]{1,0:T(8,128)(2,1)} %w_hbm.1), custom_call_target="tpu_custom_call" | custom-call | tf_op jit(solution)/shard_map/window_attention/pallas_call | solution.py:347
  50.1 0.8 %copy.7 = bf16[768,384]{1,0:T(8,128)(2,1)} copy(bf16[768,384]{1,0:T(8,128)(2,1)S(1)} %bitcast.1) | data formatting | bytes 1179648
